TPU v7x, 256 devices: a whole 4x4x8 slice. The times are simulated.
256 devices in a mesh: dp: 16 (over y, x), cluster: 16 (over z, core).
Axes of the slice: x: 4, y: 4, z: 8, core: 2. Of those that a mesh axis runs over, the one named last changes fastest.
Arguments:
- points: bfloat16 [524288, 768], P(('dp', 'cluster')), may hold values from -12 to 12
- coarse_id: int32 [524288, 1], P(('dp', 'cluster')), may hold values from 0 to 255; in each aligned block of 2048 rows (0 to 2047, 2048 to 4095, ...) at most 24 rows name the same one
- owner_map: int32 [256], replicated, may hold values from 0 to 255, each once
- centroids: bfloat16 [256, 256, 768], P('cluster', 'dp'), may hold values from -1 to 1
Outputs:
- new_centroids: bfloat16 [256, 256, 768], P('cluster', 'dp')
- point_score: float32 [524288], P(('dp', 'cluster'))
Inputs may be any that keep to these rules, and one draw needn't show every extreme that they name: `coarse_id`: in the rows of one device no coarse cluster appears more than 24 times, and some cluster appears exactly 24 times. `owner_map`: a permutation; slot s lies on cluster index s // 16.
All inputs are finite; a program needn't handle non-finite values.
Results may differ from a plain program's by a relative error of at most 0.007.
Values may be sent and summed in bfloat16 or wider, within the bound.
No kernel may reach another device: no remote copies, remote signals or barrier semaphores. Data moves between devices by JAX's collectives and lax.ppermute only.
A program may use at most 128 MiB of HBM per device.

v0:
```python
import jax
import jax.numpy as jnp
from jax import lax
from jax.sharding import PartitionSpec as P

prior_mass = 4.0


def local(points, coarse_id, owner_map, centroids):
    slots_dev = centroids.shape[0]
    feature_width = points.shape[1]
    cluster_count = lax.axis_size("cluster")
    total_slots = owner_map.shape[0]
    point_rows = points.shape[0]
    capacity = 3 * point_rows // total_slots
    coarse = coarse_id[:, 0]
    slot_ids = jnp.arange(total_slots, dtype=jnp.int32)
    lookup = coarse[:, None] == slot_ids[None, :]
    slot_index = jnp.sum(jnp.where(lookup, owner_map[None, :], 0), axis=1)
    slot_hits = (slot_index[:, None] == slot_ids[None, :]).astype(jnp.int32)
    position_in = jnp.sum((jnp.cumsum(slot_hits, 0) - 1) * slot_hits, axis=1)
    placement = slot_index * capacity + position_in
    outbound = (
        jnp.zeros((total_slots * capacity, feature_width), jnp.bfloat16).at[placement].set(points)
    )
    filled = (
        jnp.zeros((total_slots * capacity,), jnp.bfloat16)
        .at[placement]
        .set(jnp.ones((point_rows,), jnp.bfloat16))
    )
    panels = lax.all_gather(centroids, "dp", axis=1, tiled=True)
    inbound, present = (
        lax.all_to_all(outbound, "cluster", split_axis=0, concat_axis=0, tiled=True),
        lax.all_to_all(filled, "cluster", split_axis=0, concat_axis=0, tiled=True),
    )
    arrived = inbound.reshape(cluster_count, slots_dev, capacity, feature_width)
    present_mask = present.reshape(cluster_count, slots_dev, capacity)
    sqnorm = jnp.sum(jnp.square(panels.astype(jnp.float32)), -1)
    logits = (
        jnp.einsum("sjcd,jfd->sjcf", arrived, panels, preferred_element_type=jnp.float32)
        - 0.5 * sqnorm[None, :, None, :]
    )
    row_peak = jnp.max(logits, -1, keepdims=True)
    shifted = jnp.exp(logits - row_peak)
    row_total = jnp.sum(shifted, -1, keepdims=True)
    log_total = row_peak[..., 0] + jnp.log(row_total[..., 0])
    weights_bf = (shifted / row_total).astype(jnp.bfloat16) * present_mask[..., None]
    returned = lax.all_to_all(
        log_total.reshape(-1), "cluster", split_axis=0, concat_axis=0, tiled=True
    )
    point_score = returned[placement]
    weighted = jnp.einsum("sjcf,sjcd->jfd", weights_bf, arrived, preferred_element_type=jnp.float32)
    counts = jnp.sum(weights_bf.astype(jnp.float32), axis=(0, 2))
    weighted_part, counts_part = (
        lax.psum_scatter(weighted, "dp", scatter_dimension=1, tiled=True),
        lax.psum_scatter(counts, "dp", scatter_dimension=1, tiled=True),
    )
    updated = (
        (weighted_part + prior_mass * centroids.astype(jnp.float32))
        / (counts_part[..., None] + prior_mass)
    ).astype(jnp.bfloat16)
    return (updated, point_score)


def solution(mesh):
    placed = (P(("dp", "cluster"), None), P(("dp", "cluster"), None), P(), P("cluster", "dp", None))
    return jax.shard_map(
        local,
        mesh=mesh,
        in_specs=placed,
        out_specs=(P("cluster", "dp", None), P(("dp", "cluster"))),
        check_vma=False,
    )
```

profile of v0, /device:TPU:32, one launch (start us, length us, event | category | flops | bytes accessed | tf_op | source)
XLA Modules:
  0.0 407.8 jit_solution(2727471434417005122)
XLA Ops:
  7.2 1.4 select_reduce_fusion
  8.6 0.1 copy.13
  8.7 0.3 fusion.14
  9.1 0.3 add_add_fusion
  9.4 1.2 copy.14
  10.6 0.9 fusion.13
  11.6 14.6 %scatter_custom_fusion.1 = bf16[6144]{0:T(1024)(128)(2,1)S(1)} fusion(s32[2048]{0:T(1024)S(1)} %bitcast.51, bf16[2048]{0:T(1024)(128)(2,1)S(1)} %broadcast.64, bf16[]{:T(256)} %constant.10.clone.1), kind=kCustom, calls=%fused_computation.36 | custom fusion | bytes 12290 | tf_op jit(solution)/shard_map/scatter | solution.py:29
  26.2 0.5 broadcast.74
  26.7 0.7 reduce.2
  27.4 0.7 reshape.130
  28.1 8.6 %all-to-all-start.1 = ((bf16[16,2,192]{2,1,0:T(2,128)(2,1)}), bf16[16,2,192]{2,1,0:T(2,128)(2,1)S(1)}, u32[]{:S(2)}, u32[]{:S(2)}) async-start(bf16[16,2,192]{2,1,0:T(2,128)(2,1)} %reshape.130), calls=%async_computation.1 | async-start | bytes 32768 | tf_op jit(solution)/shard_map/all_to_all | solution.py:34
  36.7 15.7 %scatter_custom_fusion = bf16[6144,768]{1,0:T(8,128)(2,1)} fusion(s32[2048]{0:T(1024)S(1)} %bitcast.52, bf16[2048,768]{1,0:T(8,128)(2,1)} %param.4, bf16[]{:T(256)} %constant.10.clone.1), kind=kCustom, calls=%fused_computation.15 | custom fusion | bytes 9437696 | tf_op jit(solution)/shard_map/scatter | solution.py:24
  52.4 0.0 all-to-all-done.1
  52.4 7.2 %all-to-all-start = ((bf16[16,384,768]{2,1,0:T(8,128)(2,1)}), bf16[16,384,768]{2,1,0:T(8,128)(2,1)}, u32[]{:S(2)}, u32[]{:S(2)}) async-start(bf16[16,384,768]{2,1,0:T(8,128)(2,1)} %bitcast.47), calls=%async_computation | async-start | bytes 18874368 | tf_op jit(solution)/shard_map/all_to_all | solution.py:33
  59.6 0.0 all-gather.2.cloned.1.call-start
  59.7 0.7 all-gather.2.cloned.1.call-update
  60.3 0.0 reduce-scatter.3.cloned.1.call-start
  60.4 0.1 reshape.131
  60.5 0.1 bitcast_reduce_fusion.1
  60.6 0.1 mul.49
  60.7 69.4 %all-gather.2.cloned.1.call-done = bf16[16,256,768]{2,1,0:T(8,128)(2,1)} async-done(((bf16[16,16,768]{2,1,0:T(8,128)(2,1)}), bf16[16,256,768]{2,1,0:T(8,128)(2,1)}) %all-gather.2.cloned.1.call-update) | async-done | bytes 6291472 | tf_op jit(solution)/shard_map/all_gather | solution.py:31
  130.1 4.1 %multiply_reduce_fusion = f32[16,256]{1,0:T(8,128)S(1)} fusion(bf16[16,256,768]{2,1,0:T(8,128)(2,1)} %all-gather.2.cloned.1.call-done), kind=kLoop, calls=%fused_computation.3 | loop fusion | flops 9433088 | bytes 6307840 | tf_op jit(solution)/shard_map/reduce_sum | solution.py:38
  134.2 130.2 %all-to-all-done = bf16[16,384,768]{2,1,0:T(8,128)(2,1)} async-done(((bf16[16,384,768]{2,1,0:T(8,128)(2,1)}), bf16[16,384,768]{2,1,0:T(8,128)(2,1)}, u32[]{:S(2)}, u32[]{:S(2)}) %all-to-all-start) | async-done | bytes 9437216 | tf_op jit(solution)/shard_map/all_to_all | solution.py:33
  264.3 10.8 %bitcast_reduce_fusion = (f32[16,16,24]{2,0,1:T(8,128)S(1)}, f32[16,16,24,256]{3,2,1,0:T(8,128)}) fusion(f32[16,256]{1,0:T(8,128)S(1)} %broadcast_multiply_fusion, bf16[16,256,768]{2,1,0:T(8,128)(2,1)} %all-gather.2.cloned.1.call-done, bf16[16,16,24,768]{3,2,1,0:T(8,128)(2,1)} %bitcast.8), kind=kOutput, calls=%fused_computation.10 | convolution fusion | flops 2419058688 | bytes 22061056 | tf_op jit(solution)/shard_map/sjcd,jfd->sjcf/dot_general | solution.py:40
  275.2 0.0 copy-start
  275.2 4.3 %fusion.6 = f32[16,16,24]{2,0,1:T(8,128)S(1)} fusion(f32[16,16,24,256]{3,2,1,0:T(8,128)} %get-tuple-element.5, f32[16,16,24]{2,0,1:T(8,128)S(1)} %get-tuple-element.4, f32[16,256]{1,0:T(8,128)S(1)} %broadcast_multiply_fusion), kind=kLoop, calls=%fused_computation.14 | loop fusion | flops 4712448 | bytes 6356992 | tf_op jit(solution)/shard_map/reduce_sum | solution.py:45
  279.5 0.3 copy-done
  279.8 3.1 convert_reduce_fusion
  283.0 10.1 %fusion.9 = f32[16,256,768]{2,1,0:T(8,128)} fusion(bf16[16,16,24,256]{3,2,0,1:T(8,128)(2,1)S(1)} %get-tuple-element.3, bf16[16,16,24,768]{3,2,1,0:T(8,128)(2,1)} %bitcast.8), kind=kOutput, calls=%fused_computation.17 | convolution fusion | flops 2415919104 | bytes 25165824 | tf_op jit(solution)/shard_map/sjcf,sjcd->jfd/dot_general | solution.py:52
  293.0 0.0 copy-start.2
  293.0 0.0 reduce-scatter.3.cloned.1.call-update
  293.1 0.0 copy-start.1
  293.1 0.6 copy-done.2
  293.7 0.6 dynamic-slice
  295.0 0.7 add.64
  295.8 6.7 %all-to-all-start.2 = ((f32[16,384,1]{1,2,0:T(1,128)}), f32[16,384,1]{1,2,0:T(1,128)S(1)}, u32[]{:S(2)}, u32[]{:S(2)}) async-start(f32[16,384,1]{1,2,0:T(1,128)} %add.64), calls=%async_computation.3 | async-start | bytes 49152 | tf_op jit(solution)/shard_map/all_to_all | solution.py:48
  302.5 75.8 %all-reduce = f32[16,256]{1,0:T(8,128)S(1)} all-reduce(f32[16,256]{1,0:T(8,128)S(1)} %get-tuple-element.2), channel_id=3, replica_groups=mesh['dp'=16,'cluster'=16] {'dp'}, use_global_device_ids=true, to_apply=%region_11.12.clone | all-reduce | flops 4096 | bytes 32768
  378.3 0.1 dynamic-slice_add_fusion
  378.4 0.0 all-to-all-done.2
  378.4 20.5 %gather_fusion = f32[2048]{0:T(1024)} fusion(f32[6144]{0:T(1024)S(1)} %bitcast.46, s32[2048]{0:T(1024)S(1)} %broadcast_clamp_fusion), kind=kCustom, calls=%fused_computation | custom fusion | bytes 24576 | tf_op jit(solution)/shard_map/gather | solution.py:51
  399.0 0.0 reduce-scatter.3.cloned.1.call-done
  399.0 0.0 copy-done.1
  399.0 2.0 divide_convert_fusion.1
  (12 shorter events, 0.2 us)
Async XLA Ops:
  28.1 24.3 %all-to-all-start.1 = ((bf16[16,2,192]{2,1,0:T(2,128)(2,1)}), bf16[16,2,192]{2,1,0:T(2,128)(2,1)S(1)}, u32[]{:S(2)}, u32[]{:S(2)}) async-start(bf16[16,2,192]{2,1,0:T(2,128)(2,1)} %reshape.130), calls=%async_computation.1 | async-start | bytes 32768 | tf_op jit(solution)/shard_map/all_to_all | solution.py:34
  52.4 212.0 %all-to-all-start = ((bf16[16,384,768]{2,1,0:T(8,128)(2,1)}), bf16[16,384,768]{2,1,0:T(8,128)(2,1)}, u32[]{:S(2)}, u32[]{:S(2)}) async-start(bf16[16,384,768]{2,1,0:T(8,128)(2,1)} %bitcast.47), calls=%async_computation | async-start | bytes 18874368 | tf_op jit(solution)/shard_map/all_to_all | solution.py:33
  59.6 70.5 %all-gather.2.cloned.1.call-start = ((), (), s32[]{:S(2)}) async-start(), calls=%async_computation.4 | async-start | bytes 6684672 | tf_op jit(solution)/shard_map/all_gather | solution.py:31
  60.3 338.6 %reduce-scatter.3.cloned.1.call-start = ((), (), s32[]{:S(2)}) async-start(), calls=%async_computation.5 | async-start | bytes 13369344 | tf_op jit(solution)/shard_map/reduce_scatter | solution.py:55
  275.2 4.6 %copy-start = (f32[16,16,24,256]{3,2,1,0:T(8,128)S(1)}, f32[16,16,24,256]{3,2,1,0:T(8,128)}, u32[]{:S(2)}) copy-start(f32[16,16,24,256]{3,2,1,0:T(8,128)} %get-tuple-element.5) | copy-start | bytes 18874372
  293.0 0.7 copy-start.2
  293.1 105.9 %copy-start.1 = (bf16[16,16,768]{2,1,0:T(8,128)(2,1)S(1)}, bf16[16,16,768]{2,1,0:T(8,128)(2,1)}, u32[]{:S(2)}) copy-start(bf16[16,16,768]{2,1,0:T(8,128)(2,1)} %param.7) | copy-start | bytes 1179652
  295.8 82.6 %all-to-all-start.2 = ((f32[16,384,1]{1,2,0:T(1,128)}), f32[16,384,1]{1,2,0:T(1,128)S(1)}, u32[]{:S(2)}, u32[]{:S(2)}) async-start(f32[16,384,1]{1,2,0:T(1,128)} %add.64), calls=%async_computation.3 | async-start | bytes 49152 | tf_op jit(solution)/shard_map/all_to_all | solution.py:48
Sparse Core Ops, SparseCore 0:
  62.8 67.1 all-gather.1
  293.2 101.0 reduce-scatter.2
where the time goes:
time: 408 us
  waiting for transfers between devices  200 us (49%)
  blocking collectives  75.8 us (19%)
  local copies, waits for them, and re-layouts  56.1 us (14%)
  starting transfers between devices  22.6 us (6%)
  matrix products  20.9 us (5%)
  other arithmetic  17.3 us (4%)
  between operations  14.9 us (4%)
    all_to_all x1, waiting for transfers between devices, local(): lax.all_to_all(outbound, 'cluster', split_axis=0, concat_axis=0, tiled=True)  130 us
    unnamed x1, blocking collectives  75.8 us
    all_gather x1, waiting for transfers between devices, local(): panels = lax.all_gather(centroids, 'dp', axis=1, tiled=True)  69.4 us
    gather x1, local copies, waits for them, and re-layouts, local(): point_score = returned[placement]  20.5 us
    scatter x1, local copies, waits for them, and re-layouts, local(): jnp.zeros((total_slots * capacity, feature_width), jnp.bfloat16)  15.7 us
    scatter x1, local copies, waits for them, and re-layouts, local(): filled = jnp.zeros((total_slots * capacity,), jnp.bfloat16).at[placement]...  14.6 us
    dot_general x1, matrix products, local(): jnp.einsum('sjcd,jfd->sjcf', arrived, panels, preferred_element_type=jnp....  10.8 us
    dot_general x1, matrix products, local(): jnp.einsum('sjcf,sjcd->jfd', weights_bf, arrived, preferred_element_type=...  10.1 us
  transfers between devices with their start and end apart: 5, of which 2 were waited for; matrix products, arithmetic and copies ran while one was open for 10% of the time, Pallas kernels for 0%

commit v1 on v0

--- a/solution.py
+++ b/solution.py
@@ -28,7 +28,10 @@
         .at[placement]
         .set(jnp.ones((point_rows,), jnp.bfloat16))
     )
-    panels = lax.all_gather(centroids, "dp", axis=1, tiled=True)
+    everything = lax.psum(1, "dp")
+    small = jnp.stack([centroids] * everything)
+    big = lax.all_to_all(small, "dp", 0, 0)
+    panels = jnp.concatenate(big, axis=1)
     inbound, present = (
         lax.all_to_all(outbound, "cluster", split_axis=0, concat_axis=0, tiled=True),
         lax.all_to_all(filled, "cluster", split_axis=0, concat_axis=0, tiled=True),

time: 408 us -> 499 us (1.22)
  waiting for transfers between devices: 200 us -> 272 us
  blocking collectives: 75.8 us -> 87.7 us
  local copies, waits for them, and re-layouts: 56.1 us -> 65.1 us
    all_to_all x1, waiting for transfers between devices: 0.01 us -> 78.4 us  [local(): big = lax.all_to_all(small, 'dp', 0, 0)]
    all_gather x1 -> x0, waiting for transfers between devices: 69.4 us -> none  [local(): panels = lax.all_gather(centroids, 'dp', axis=1, tiled=True)]
    all_to_all x1, waiting for transfers between devices: 130 us -> 194 us  [local(): lax.all_to_all(outbound, 'cluster', split_axis=0, concat_axis=0, tiled=True)]
    all_to_all x0 -> x1, blocking collectives: none -> 14.6 us  [local(): lax.all_to_all(filled, 'cluster', split_axis=0, concat_axis=0, tiled=True)]
    reshape x0 -> x1, local copies, waits for them, and re-layouts: none -> 6.19 us  [local(): panels = jnp.concatenate(big, axis=1)]
  transfers between devices with their start and end apart: 5 -> 4, of which waited for: 2 -> 2; matrix products, arithmetic and copies ran while one was open for 10% -> 10% of each run, Pallas kernels for 0% -> 0%
where the time goes in v1:
time: 499 us; the launch traced here: 498 us
  waiting for transfers between devices  272 us (55%)
  blocking collectives  87.7 us (18%)
  local copies, waits for them, and re-layouts  65.1 us (13%)
  matrix products  20.9 us (4%)
  starting transfers between devices  20.1 us (4%)
  other arithmetic  17.3 us (3%)
  between operations  14.9 us (3%)
    all_to_all x1, waiting for transfers between devices, local(): lax.all_to_all(outbound, 'cluster', split_axis=0, concat_axis=0, tiled=True)  194 us
    all_to_all x1, waiting for transfers between devices, local(): big = lax.all_to_all(small, 'dp', 0, 0)  78.4 us
    unnamed x1, blocking collectives  73.1 us
    gather x1, local copies, waits for them, and re-layouts, local(): point_score = returned[placement]  20.5 us
    scatter x1, local copies, waits for them, and re-layouts, local(): jnp.zeros((total_slots * capacity, feature_width), jnp.bfloat16)  15.7 us
    all_to_all x1, blocking collectives, local(): lax.all_to_all(filled, 'cluster', split_axis=0, concat_axis=0, tiled=True)  14.6 us
    scatter x1, local copies, waits for them, and re-layouts, local(): filled = jnp.zeros((total_slots * capacity,), jnp.bfloat16).at[placement]...  14.6 us
    dot_general x1, matrix products, local(): jnp.einsum('sjcd,jfd->sjcf', arrived, panels, preferred_element_type=jnp....  10.8 us
  transfers between devices with their start and end apart: 4, of which 2 were waited for; matrix products, arithmetic and copies ran while one was open for 10% of the time, Pallas kernels for 0%

profile of v1, /device:TPU:32, one launch (start us, length us, event | category | flops | bytes accessed | tf_op | source)
XLA Modules:
  0.0 498.1 jit_solution(5344813668684489611)
XLA Ops:
  7.2 1.4 select_reduce_fusion
  8.6 0.1 copy.31
  8.7 0.0 copy-start.1
  8.7 0.3 fusion.13
  9.1 0.3 add_add_fusion
  9.4 1.2 copy.32
  10.6 0.9 fusion.12
  11.6 14.6 %scatter_custom_fusion.1 = bf16[6144]{0:T(1024)(128)(2,1)S(1)} fusion(s32[2048]{0:T(1024)S(1)} %bitcast.53, bf16[2048]{0:T(1024)(128)(2,1)S(1)} %broadcast.68, bf16[]{:T(256)} %constant.10.clone.1), kind=kCustom, calls=%fused_computation.35 | custom fusion | bytes 12290 | tf_op jit(solution)/shard_map/scatter | solution.py:29
  26.2 0.5 broadcast.78
  26.7 0.7 reduce.3
  27.4 0.1 reshape.146
  27.5 14.6 %all_to_all.33 = bf16[16,2,192]{2,1,0:T(2,128)(2,1)S(1)} all-to-all(bf16[16,2,192]{2,1,0:T(2,128)(2,1)S(1)} %reshape.146), channel_id=1, replica_groups=mesh['dp'=16,'cluster'=16] {'cluster'}, dimensions={0} | all-to-all | bytes 24576 | tf_op jit(solution)/shard_map/all_to_all | solution.py:37
  42.1 0.0 copy-done.1
  42.1 3.3 stack.2
  45.4 7.1 %all-to-all-start.1 = ((bf16[16,16,16,768]{3,2,1,0:T(8,128)(2,1)}), bf16[16,16,16,768]{3,2,1,0:T(8,128)(2,1)}, u32[]{:S(2)}, u32[]{:S(2)}) async-start(bf16[16,16,16,768]{3,2,1,0:T(8,128)(2,1)} %stack.2), calls=%async_computation.1 | async-start | bytes 12582912 | tf_op jit(solution)/shard_map/all_to_all | solution.py:33
  52.5 15.7 %scatter_custom_fusion = bf16[6144,768]{1,0:T(8,128)(2,1)} fusion(s32[2048]{0:T(1024)S(1)} %bitcast.54, bf16[2048,768]{1,0:T(8,128)(2,1)} %param.4, bf16[]{:T(256)} %constant.10.clone.1), kind=kCustom, calls=%fused_computation.14 | custom fusion | bytes 9437696 | tf_op jit(solution)/shard_map/scatter | solution.py:24
  68.2 78.4 %all-to-all-done.1 = bf16[16,16,16,768]{3,2,1,0:T(8,128)(2,1)} async-done(((bf16[16,16,16,768]{3,2,1,0:T(8,128)(2,1)}), bf16[16,16,16,768]{3,2,1,0:T(8,128)(2,1)}, u32[]{:S(2)}, u32[]{:S(2)}) %all-to-all-start.1) | async-done | bytes 6291488 | tf_op jit(solution)/shard_map/all_to_all | solution.py:33
  146.6 6.0 %all-to-all-start = ((bf16[16,384,768]{2,1,0:T(8,128)(2,1)}), bf16[16,384,768]{2,1,0:T(8,128)(2,1)}, u32[]{:S(2)}, u32[]{:S(2)}) async-start(bf16[16,384,768]{2,1,0:T(8,128)(2,1)} %bitcast.48), calls=%async_computation | async-start | bytes 18874368 | tf_op jit(solution)/shard_map/all_to_all | solution.py:36
  152.6 0.3 reduce-scatter.3.cloned.1.call-start
  152.8 0.1 reshape.147
  152.9 0.1 bitcast_reduce_fusion.1
  153.0 0.1 mul.53
  153.2 4.1 multiply_reduce_fusion
  157.3 0.1 mul.52
  157.4 6.2 %copy.33 = bf16[16,16,16,768]{3,2,1,0:T(8,128)(2,1)} copy(bf16[16,16,16,768]{3,2,0,1:T(8,128)(2,1)} %bitcast.9) | data formatting | bytes 12582912 | tf_op jit(solution)/shard_map/reshape | solution.py:34
  163.6 193.7 %all-to-all-done = bf16[16,384,768]{2,1,0:T(8,128)(2,1)} async-done(((bf16[16,384,768]{2,1,0:T(8,128)(2,1)}), bf16[16,384,768]{2,1,0:T(8,128)(2,1)}, u32[]{:S(2)}, u32[]{:S(2)}) %all-to-all-start) | async-done | bytes 9437216 | tf_op jit(solution)/shard_map/all_to_all | solution.py:36
  357.3 10.8 %bitcast_reduce_fusion = (f32[16,16,24]{2,0,1:T(8,128)S(1)}, f32[16,16,24,256]{3,2,1,0:T(8,128)}) fusion(f32[16,256]{1,0:T(8,128)S(1)} %mul.52, bf16[16,256,768,1]{2,1,3,0:T(8,128)(2,1)} %bitcast.49, bf16[16,16,24,768]{3,2,1,0:T(8,128)(2,1)} %bitcast.8), kind=kOutput, calls=%fused_computation.9 | convolution fusion | flops 2419058688 | bytes 22061056 | tf_op jit(solution)/shard_map/sjcd,jfd->sjcf/dot_general | solution.py:43
  368.1 0.0 copy-start
  368.1 4.3 fusion.5
  372.4 0.3 copy-done
  372.8 3.1 convert_reduce_fusion
  375.9 10.1 %fusion.8 = f32[16,256,768]{2,1,0:T(8,128)} fusion(bf16[16,16,24,256]{3,2,0,1:T(8,128)(2,1)S(1)} %get-tuple-element.3, bf16[16,16,24,768]{3,2,1,0:T(8,128)(2,1)} %bitcast.8), kind=kOutput, calls=%fused_computation.16 | convolution fusion | flops 2415919104 | bytes 25165824 | tf_op jit(solution)/shard_map/sjcf,sjcd->jfd/dot_general | solution.py:55
  386.0 0.0 copy-start.2
  386.0 0.0 reduce-scatter.3.cloned.1.call-update
  386.0 0.6 copy-done.2
  386.7 0.6 dynamic-slice
  388.0 0.7 add.64
  388.8 6.8 %all-to-all-start.3 = ((f32[16,384,1]{1,2,0:T(1,128)}), f32[16,384,1]{1,2,0:T(1,128)S(1)}, u32[]{:S(2)}, u32[]{:S(2)}) async-start(f32[16,384,1]{1,2,0:T(1,128)} %add.64), calls=%async_computation.4 | async-start | bytes 49152 | tf_op jit(solution)/shard_map/all_to_all | solution.py:51
  395.5 73.1 %all-reduce = f32[16,256]{1,0:T(8,128)S(1)} all-reduce(f32[16,256]{1,0:T(8,128)S(1)} %get-tuple-element.2), channel_id=3, replica_groups=mesh['dp'=16,'cluster'=16] {'dp'}, use_global_device_ids=true, to_apply=%region_11.12.clone | all-reduce | flops 4096 | bytes 32768
  468.6 0.1 dynamic-slice_add_fusion
  468.7 0.0 all-to-all-done.3
  468.7 20.5 %gather_fusion = f32[2048]{0:T(1024)} fusion(f32[6144]{0:T(1024)S(1)} %bitcast.47, s32[2048]{0:T(1024)S(1)} %broadcast_clamp_fusion), kind=kCustom, calls=%fused_computation | custom fusion | bytes 24576 | tf_op jit(solution)/shard_map/gather | solution.py:54
  489.2 0.0 reduce-scatter.3.cloned.1.call-done
  489.2 2.0 divide_convert_fusion.1
  (13 shorter events, 0.2 us)
Async XLA Ops:
  8.7 33.4 %copy-start.1 = (bf16[16,16,768]{2,1,0:T(8,128)(2,1)S(1)}, bf16[16,16,768]{2,1,0:T(8,128)(2,1)}, u32[]{:S(2)}) copy-start(bf16[16,16,768]{2,1,0:T(8,128)(2,1)} %param.7) | copy-start | bytes 1179652
  45.4 101.2 %all-to-all-start.1 = ((bf16[16,16,16,768]{3,2,1,0:T(8,128)(2,1)}), bf16[16,16,16,768]{3,2,1,0:T(8,128)(2,1)}, u32[]{:S(2)}, u32[]{:S(2)}) async-start(bf16[16,16,16,768]{3,2,1,0:T(8,128)(2,1)} %stack.2), calls=%async_computation.1 | async-start | bytes 12582912 | tf_op jit(solution)/shard_map/all_to_all | solution.py:33
  146.6 210.7 %all-to-all-start = ((bf16[16,384,768]{2,1,0:T(8,128)(2,1)}), bf16[16,384,768]{2,1,0:T(8,128)(2,1)}, u32[]{:S(2)}, u32[]{:S(2)}) async-start(bf16[16,384,768]{2,1,0:T(8,128)(2,1)} %bitcast.48), calls=%async_computation | async-start | bytes 18874368 | tf_op jit(solution)/shard_map/all_to_all | solution.py:36
  152.6 336.7 %reduce-scatter.3.cloned.1.call-start = ((), (), s32[]{:S(2)}) async-start(), calls=%async_computation.5 | async-start | bytes 13369344 | tf_op jit(solution)/shard_map/reduce_scatter | solution.py:58
  368.1 4.6 copy-start
  386.0 0.7 copy-start.2
  388.8 79.9 %all-to-all-start.3 = ((f32[16,384,1]{1,2,0:T(1,128)}), f32[16,384,1]{1,2,0:T(1,128)S(1)}, u32[]{:S(2)}, u32[]{:S(2)}) async-start(f32[16,384,1]{1,2,0:T(1,128)} %add.64), calls=%async_computation.4 | async-start | bytes 49152 | tf_op jit(solution)/shard_map/all_to_all | solution.py:51
Sparse Core Ops, SparseCore 0:
  386.1 99.3 reduce-scatter.2
